TPU v7x, 32 devices: a whole 2x2x4 slice. The times are simulated.
32 devices in a mesh: section: 2 (over core), ctx: 4 (over z), mp: 4 (over y, x).
Axes of the slice: x: 2, y: 2, z: 4, core: 2. Of those that a mesh axis runs over, the one named last changes fastest.
Arguments:
- frames: bfloat16 [2, 16, 128, 512], P('section', 'ctx'), may hold values from -6 to 6
- w_conv: bfloat16 [3, 512, 512], replicated, may hold values from -0.15625 to 0.15625
- w_lat: bfloat16 [512, 16], replicated, may hold values from -0.25 to 0.25
- dest: int32 [2, 512, 1], P(None, 'ctx'), may hold values from 0 to 3; in each aligned block of 128 rows (0 to 127, 128 to 255, ..., all dimensions but the last counted through in order) at most 48 rows name the same one
- pick: int32 [2, 512], P(None, 'ctx'), may hold values from 0 to 6
- w_embed: bfloat16 [64, 6144], replicated, may hold values from -0.75 to 0.75
- gain: float32 [6144], replicated, may hold values from 0.25 to 1.75
- w_qkv: bfloat16 [6144, 3, 4096], P(None, None, 'mp'), may hold values from -0.078125 to 0.078125
Outputs:
- attended: bfloat16 [2, 768, 4096], P('section', 'ctx', 'mp')
Inputs may be any that keep to these rules, and one draw needn't show every extreme that they name: `dest`: among the 128 rows of one frame block, at most 48 name the same context shard, and some frame block reaches 48.
All inputs are finite; a program needn't handle non-finite values.
Results may differ from a plain program's by a relative error of at most 0.0061.
Values may be sent and summed in bfloat16 or wider, within the bound.
A program may use at most 128 MiB of HBM per device.

v0:
```python
import functools

import jax
import jax.numpy as jnp
from jax import lax
from jax.experimental import pallas as pl
from jax.experimental.pallas import tpu as pltpu
from jax.sharding import PartitionSpec as P

HEAD = 128
GROUP = 4
LANES = 128
META = 16
EPS = 1e-06
SPLIT = True
MESH = pl.DeviceIdType.MESH
F32 = jnp.float32
BF16 = jnp.bfloat16
HBM = pl.BlockSpec(memory_space=pltpu.HBM)


def dot(a, b):
    return jnp.dot(a, b, preferred_element_type=F32)


def dot_nt(a, b):
    return lax.dot_general(a, b, (((1,), (1,)), ((), ())), preferred_element_type=F32)


def iota(shape, dim):
    return lax.broadcasted_iota(jnp.int32, shape, dim)


def encode_kernel(
    shards, frame_count, pieces, split,
    frames_hbm, conv_hbm, lat_hbm, dest_hbm, pick_hbm, embed_hbm, gain_hbm, qkv_hbm,
    rows_out, weff_out,
    frames, conv, lat_ref, dest_ref, pick_ref, embed, gain_ref, qkv, scaled, hidden, outgoing, mine, total,
    in_sem, qkv_sem, row_send, row_recv, half_send, half_recv, keep_sem,
):
    section = lax.axis_index("section")
    ctx = lax.axis_index("ctx")
    other = 1 - section
    depth = embed.shape[1]
    latent = embed.shape[0]
    half = qkv.shape[2]
    step = depth // pieces
    row_count = outgoing.shape[0] - META

    loads = [
        pltpu.make_async_copy(source, target, in_sem.at[i])
        for i, (source, target) in enumerate((
            (embed_hbm, embed), (gain_hbm, gain_ref), (dest_hbm, dest_ref), (pick_hbm, pick_ref),
            (frames_hbm, frames), (conv_hbm, conv), (lat_hbm, lat_ref),
        ))
    ]
    for load in loads:
        load.start()
    columns = pl.ds(pl.multiple_of(section * half, LANES), half)

    def stream(j, p):
        part = pl.ds(pl.multiple_of(p * step, step), step)
        return pltpu.make_async_copy(
            qkv_hbm.at[j, part, columns], qkv.at[j, part, :], qkv_sem.at[j * pieces + p]
        )


    barrier = pltpu.get_barrier_semaphore()
    for d in range(shards):
        pl.semaphore_signal(
            barrier, inc=1,
            device_id={"section": other, "ctx": lax.rem(ctx + d, shards)}, device_id_type=MESH,
        )

    loads[0].wait()
    loads[1].wait()
    tile = 512

    def scale_part(k, carry):
        part = pl.ds(pl.multiple_of(k * tile, tile), tile)
        full = embed[:, part].astype(F32) * gain_ref[:, part]
        top = full.astype(BF16)
        scaled[:latent, part] = top
        if split:
            scaled[latent:, part] = (full - top.astype(F32)).astype(BF16)
        return carry

    lax.fori_loop(0, depth // tile, scale_part, 0)

    for load in loads[2:]:
        load.wait()
    for j in range(3):
        for p in range(pieces):
            stream(j, p).start()
    first = section == 0
    dest = jnp.where(first, dest_ref[0], dest_ref[1])
    pick = jnp.where(first, pick_ref[0:1, :], pick_ref[1:2, :])
    tier = (pick >= 4).astype(jnp.int32) + (pick >= 6).astype(jnp.int32)
    label = dest // GROUP + shards // GROUP * tier + 1
    padded = -(-shards // 8) * 8
    onehot = (iota((padded, row_count), 0) == dest).astype(F32)
    earlier = (iota((row_count, row_count), 0) < iota((row_count, row_count), 1)).astype(F32)
    before = dot(onehot.astype(BF16), earlier.astype(BF16))
    within = jnp.sum(before * onehot, axis=0, keepdims=True)
    line = iota((META, row_count), 0)
    meta = jnp.where(line == 0, dest.astype(F32), 0.0)
    meta = jnp.where(line == 1, within, meta)
    meta = jnp.where(line == 2, label.astype(F32), meta)
    outgoing[row_count:, :] = meta.astype(BF16)

    cells = frames.shape[0]
    frame = cells // frame_count
    hidden[...] = dot(frames[...], conv[0])
    hidden[frame:, :] += dot(frames[: cells - frame, :], conv[1])
    hidden[2 * frame :, :] += dot(frames[: cells - 2 * frame, :], conv[2])
    value = hidden[...]
    active = (value * jax.nn.sigmoid(value)).astype(BF16)
    channels = lat_ref.shape[0]
    per = latent // channels
    narrow = dot_nt(active, lat_ref[...]).astype(BF16)
    lane = iota((channels, LANES), 1)
    spread = ((lane % channels == iota((channels, LANES), 0)) & (lane < latent)).astype(F32)
    wide = dot(narrow, spread.astype(BF16))
    wide = jnp.where(
        iota((cells, LANES), 1) // channels == iota((cells, LANES), 0) % per, wide, 0.0
    ).astype(BF16)
    gather = (iota((row_count, cells), 1) // per == iota((row_count, cells), 0)).astype(F32)
    patches = dot(gather.astype(BF16), wide)
    narrow_patches = patches[:, :latent].astype(BF16)

    def norm_part(k, square):
        x = dot(narrow_patches, embed[:, pl.ds(pl.multiple_of(k * tile, tile), tile)])
        x = x * x
        for i in range(tile // LANES):
            square = square + x[:, i * LANES : (i + 1) * LANES]
        return square

    square = lax.fori_loop(0, depth // tile, norm_part, jnp.zeros((row_count, LANES), F32))
    scale = lax.rsqrt(jnp.sum(square, axis=1, keepdims=True) / depth + EPS)
    high = scale.astype(BF16).astype(F32)
    middle = (scale - high).astype(BF16).astype(F32)
    low = scale - high - middle
    lane = iota((row_count, LANES), 1)
    line = iota((row_count, LANES), 0)
    placed = jnp.where(line == latent + 3, label, 0).astype(F32).astype(BF16)
    message = patches + dot_nt((line == lane).astype(F32).astype(BF16), placed)
    message = jnp.where(lane == latent, high, message)
    message = jnp.where(lane == latent + 1, middle, message)
    message = jnp.where(lane == latent + 2, low, message)
    outgoing[:row_count, :] = message.astype(BF16)

    pl.semaphore_wait(barrier, shards)
    sends = []
    for d in range(shards):
        send = pltpu.make_async_remote_copy(
            src_ref=outgoing, dst_ref=rows_out.at[ctx],
            send_sem=row_send.at[d], recv_sem=row_recv.at[d],
            device_id={"section": other, "ctx": lax.rem(ctx + d, shards)}, device_id_type=MESH,
        )
        send.start()
        sends.append(send)

    def swap(j):
        return pltpu.make_async_remote_copy(
            src_ref=mine.at[j], dst_ref=weff_out.at[section, j],
            send_sem=half_send.at[j], recv_sem=half_recv.at[j],
            device_id={"section": other}, device_id_type=MESH,
        )

    def keep(j):
        return pltpu.make_async_copy(mine.at[j], weff_out.at[section, j], keep_sem.at[j])

    def contract(j, carry):
        total[...] = jnp.zeros_like(total)

        def piece(p, inner):
            stream(j, p).wait()
            part = pl.ds(pl.multiple_of(p * step, step), step)
            total[...] += dot(scaled[:, part], qkv[j, part, :])
            return inner

        lax.fori_loop(0, pieces, piece, 0)
        full = total[...]
        if split:
            full = full[:latent] + full[latent:]
        mine[j] = full.astype(BF16)
        swap(j).start()
        keep(j).start()
        return carry

    lax.fori_loop(0, 3, contract, 0)
    for send in sends:
        send.wait()
    for j in range(3):
        keep(j).wait()
        swap(j).wait()


def attend_kernel(shards, capacity, rows_ref, weff_ref, out_ref, picked_ref, row_ref, mask_ref):
    ctx = lax.axis_index("ctx")
    row_count = rows_ref.shape[1] - META
    latent = weff_ref.shape[2]
    half = weff_ref.shape[3]
    slots = out_ref.shape[0]
    total_rows = shards * row_count

    @pl.when(pl.program_id(0) == 0)
    def _():
        labels, spots = [], []
        for source in range(shards):
            meta = rows_ref[source, row_count:, :].astype(F32)
            labels.append(meta[2:3, :])
            home = meta[1:2, :] + (source * capacity)
            spots.append(jnp.where(meta[0:1, :] == ctx.astype(F32), home, -1.0))
            row_ref[source * row_count : (source + 1) * row_count, :] = rows_ref[source, :row_count, :]
        label = jnp.concatenate(labels, axis=1)
        spot = jnp.concatenate(spots, axis=1).astype(jnp.int32)
        taken = spot == iota((slots, total_rows), 0)
        picked_ref[...] = dot(taken.astype(F32).astype(BF16), row_ref[...]).astype(BF16)
        own = jnp.sum(jnp.where(taken, label, 0.0), axis=1, keepdims=True)
        mask_ref[...] = (label == own).astype(F32)

    def scale_of(block):
        return (
            block[:, latent : latent + 1].astype(F32)
            + block[:, latent + 1 : latent + 2].astype(F32)
            + block[:, latent + 2 : latent + 3].astype(F32)
        )

    def head_norm(x):
        return x * lax.rsqrt(jnp.mean(x * x, axis=-1, keepdims=True) + EPS)

    picked = picked_ref[...]
    everything = row_ref[...]
    picked_scale = scale_of(picked)
    row_scale = scale_of(everything)
    q = dot(picked[:, :latent], weff_ref[0, 0])
    k = dot(everything[:, :latent], weff_ref[0, 1])
    v = dot(everything[:, :latent], weff_ref[0, 2])
    allowed = mask_ref[...] > 0.5
    factor = 1.0 / HEAD**0.5
    for h in range(half // HEAD):
        part = slice(h * HEAD, (h + 1) * HEAD)
        queries = head_norm(q[:, part] * picked_scale).astype(BF16)
        keys = head_norm(k[:, part] * row_scale).astype(BF16)
        values = (v[:, part] * row_scale).astype(BF16)
        scores = dot_nt(queries, keys) * factor
        expo = jnp.where(allowed, jnp.exp(scores), 0.0)
        den = jnp.sum(expo, axis=1, keepdims=True)
        summed = dot(expo.astype(BF16), values)
        out_ref[:, part] = (summed / jnp.where(den > 0.0, den, 1.0)).astype(BF16)


def on_device(shards, sections, frames, w_conv, w_lat, dest, pick, w_embed, gain, w_qkv):
    _, frame_count, frame, channels = frames.shape
    latent, depth = w_embed.shape
    cells = frame_count * frame
    row_count = dest.shape[1]
    columns = w_qkv.shape[2]
    half = columns // sections
    pieces = 4
    split = SPLIT
    capacity = max(2, 3 * row_count // (2 * shards))
    slots = shards * capacity
    rows, weff = pl.pallas_call(
        functools.partial(encode_kernel, shards, frame_count, pieces, split),
        out_shape=(
            jax.ShapeDtypeStruct((shards, row_count + META, LANES), BF16),
            jax.ShapeDtypeStruct((sections, 3, latent, half), BF16),
        ),
        in_specs=[HBM] * 8,
        out_specs=(HBM, HBM),
        scratch_shapes=[
            pltpu.VMEM((cells, channels), BF16),
            pltpu.VMEM(w_conv.shape, BF16),
            pltpu.VMEM((w_lat.shape[1], channels), BF16),
            pltpu.VMEM((sections, 1, row_count), jnp.int32),
            pltpu.VMEM((sections, row_count), jnp.int32),
            pltpu.VMEM((latent, depth), BF16),
            pltpu.VMEM((1, depth), F32),
            pltpu.VMEM((3, depth, half), BF16),
            pltpu.VMEM((2 * latent if split else latent, depth), BF16),
            pltpu.VMEM((cells, channels), F32),
            pltpu.VMEM((row_count + META, LANES), BF16),
            pltpu.VMEM((3, latent, half), BF16),
            pltpu.VMEM((2 * latent if split else latent, half), F32),
            pltpu.SemaphoreType.DMA((7,)),
            pltpu.SemaphoreType.DMA((3 * pieces,)),
            pltpu.SemaphoreType.DMA((shards,)),
            pltpu.SemaphoreType.DMA((shards,)),
            pltpu.SemaphoreType.DMA((3,)),
            pltpu.SemaphoreType.DMA((3,)),
            pltpu.SemaphoreType.DMA((3,)),
        ],
        compiler_params=pltpu.CompilerParams(
            collective_id=0, has_side_effects=True, vmem_limit_bytes=67043328
        ),
    )(
        frames.reshape(cells, channels),
        w_conv,
        w_lat.T,
        dest.transpose(0, 2, 1),
        pick,
        w_embed,
        gain.reshape(1, depth),
        w_qkv.transpose(1, 0, 2),
    )
    out = pl.pallas_call(
        functools.partial(attend_kernel, shards, capacity),
        grid=(sections,),
        out_shape=jax.ShapeDtypeStruct((slots, columns), BF16),
        in_specs=[
            pl.BlockSpec((shards, row_count + META, LANES), lambda i: (0, 0, 0)),
            pl.BlockSpec((1, 3, latent, half), lambda i: (i, 0, 0, 0)),
        ],
        out_specs=pl.BlockSpec((slots, half), lambda i: (0, i)),
        scratch_shapes=[
            pltpu.VMEM((slots, LANES), BF16),
            pltpu.VMEM((shards * row_count, LANES), BF16),
            pltpu.VMEM((slots, shards * row_count), F32),
        ],
        compiler_params=pltpu.CompilerParams(vmem_limit_bytes=67043328),
    )(rows, weff)
    return out.reshape(1, slots, columns)


def solution(mesh):
    in_specs = (
        P("section", "ctx", None, None),
        P(),
        P(),
        P(None, "ctx", None),
        P(None, "ctx"),
        P(),
        P(),
        P(None, None, "mp"),
    )
    return jax.shard_map(
        functools.partial(on_device, mesh.shape["ctx"], mesh.shape["section"]),
        mesh=mesh,
        in_specs=in_specs,
        out_specs=P("section", "ctx", "mp"),
        check_vma=False,
    )
```

profile of v0, /device:TPU:1, one launch (start us, length us, event | category | flops | bytes accessed | tf_op | source)
XLA Modules:
  0.0 17.8 jit_solution(16857916862454730403)
XLA Ops:
  0.0 12.4 %shard_map.82 = (bf16[4,144,128]{2,1,0:T(8,128)(2,1)}, bf16[2,3,64,512]{3,2,1,0:T(8,128)(2,1)}) custom-call(bf16[512,512]{1,0:T(8,128)(2,1)} %bitcast.7, bf16[3,512,512]{2,1,0:T(8,128)(2,1)} %conv_hbm.1, bf16[16,512]{1,0:T(8,128)(2,1)} %bitcast.9, s32[2,1,128]{2,1,0:T(1,128)} %bitcast.10, s32[2,128]{1,0:T(2,128)} %pick_hbm.1, bf16[64,6144]{1,0:T(8,128)(2,1)} %embed_hbm.1, ...), custom_call_target="tpu_custom_call" | custom-call | tf_op jit(solution)/shard_map/pallas_call | solution.py:265
  12.4 5.3 %shard_map.83 = bf16[192,1024]{1,0:T(8,128)(2,1)} custom-call(bf16[4,144,128]{2,1,0:T(8,128)(2,1)} %get-tuple-element.7.rows_ref, bf16[2,3,64,512]{3,2,1,0:T(8,128)(2,1)} %get-tuple-element.8.weff_ref), custom_call_target="tpu_custom_call" | custom-call | tf_op jit(solution)/shard_map/pallas_call | solution.py:308
where the time goes:
time: 17.9 us; the launch traced here: 17.8 us
  Pallas kernels  17.7 us (99%)
    pallas_call x1, Pallas kernels, on_device(): pl.pallas_call(functools.partial(encode_kernel, shards, frame_count, piec...  12.4 us
    pallas_call x1, Pallas kernels, on_device(): pl.pallas_call(functools.partial(attend_kernel, shards, capacity), grid=(...  5.33 us

commit v1 on v0

v1 whole, which is shorter than its diff:
```python
import functools

import jax
import jax.numpy as jnp
from jax import lax
from jax.experimental import pallas as pl
from jax.experimental.pallas import tpu as pltpu
from jax.sharding import PartitionSpec as P

HEAD = 128
GROUP = 4
LANES = 128
META = 16
EPS = 1e-06
MESH = pl.DeviceIdType.MESH
F32 = jnp.float32
BF16 = jnp.bfloat16
HBM = pl.BlockSpec(memory_space=pltpu.HBM)
VMEM = pl.BlockSpec(memory_space=pltpu.VMEM)
LIMIT = 60 * 1024 * 1024


def dot(a, b):
    return jnp.dot(a, b, preferred_element_type=F32)


def dot_nt(a, b):
    return lax.dot_general(a, b, (((1,), (1,)), ((), ())), preferred_element_type=F32)


def iota(shape, dim):
    return lax.broadcasted_iota(jnp.int32, shape, dim)


def encode_kernel(
    shards, frame_count, pieces,
    frames_hbm, conv_hbm, lat_hbm, dest_hbm, pick_hbm, embed_hbm, gain_hbm, qkv_hbm,
    rows_out, meta_out, weff_out,
    frames, conv, lat_ref, dest_ref, pick_ref, embed, gain_ref, qkv, scaled, wide, packed, meta_ref, total,
    in_sem, qkv_sem, row_send, row_recv, meta_send, meta_recv, half_send, half_recv,
):
    section = lax.axis_index("section")
    ctx = lax.axis_index("ctx")
    other = 1 - section
    depth = embed.shape[1]
    latent = embed.shape[0]
    half = qkv.shape[2]
    step = depth // pieces
    row_count = dest_ref.shape[2]
    pack = LANES // latent
    lines = row_count // pack

    barrier = pltpu.get_barrier_semaphore()
    for d in range(shards):
        pl.semaphore_signal(
            barrier, inc=1,
            device_id={"section": other, "ctx": lax.rem(ctx + d, shards)}, device_id_type=MESH,
        )
    loads = [
        pltpu.make_async_copy(source, target, in_sem.at[i])
        for i, (source, target) in enumerate((
            (dest_hbm, dest_ref), (pick_hbm, pick_ref), (lat_hbm, lat_ref),
            (frames_hbm, frames), (conv_hbm, conv), (embed_hbm, embed), (gain_hbm, gain_ref),
        ))
    ]
    for load in loads:
        load.start()
    columns = pl.ds(pl.multiple_of(section * half, LANES), half)

    def stream(j, p):
        part = pl.ds(pl.multiple_of(p * step, step), step)
        return pltpu.make_async_copy(
            qkv_hbm.at[j, part, columns], qkv.at[j, part, :], qkv_sem.at[j * pieces + p]
        )

    for j in range(3):
        for p in range(pieces):
            stream(j, p).start()

    def target(d):
        return {"section": other, "ctx": lax.rem(ctx + d, shards)}

    order = sorted(range(shards), key=lambda d: -min(d, shards - d))

    loads[0].wait()
    loads[1].wait()
    first = section == 0
    dest = jnp.where(first, dest_ref[0], dest_ref[1])
    pick = jnp.where(first, pick_ref[0:1, :], pick_ref[1:2, :])
    tier = (pick >= 4).astype(jnp.int32) + (pick >= 6).astype(jnp.int32)
    label = dest // GROUP + shards // GROUP * tier + 1
    padded = -(-shards // 8) * 8
    onehot = (iota((padded, row_count), 0) == dest).astype(F32)
    earlier = (iota((row_count, row_count), 0) < iota((row_count, row_count), 1)).astype(F32)
    before = dot(onehot.astype(BF16), earlier.astype(BF16))
    within = jnp.sum(before * onehot, axis=0, keepdims=True)
    line = iota((META, row_count), 0)
    meta = jnp.where(line == 0, dest.astype(F32), 0.0)
    meta = jnp.where(line == 1, within, meta)
    meta = jnp.where(line == 2, label.astype(F32), meta)
    meta_ref[...] = meta.astype(BF16)
    pl.semaphore_wait(barrier, shards)
    sends = []
    for d in order:
        send = pltpu.make_async_remote_copy(
            src_ref=meta_ref, dst_ref=meta_out.at[ctx],
            send_sem=meta_send.at[d], recv_sem=meta_recv.at[d],
            device_id=target(d), device_id_type=MESH,
        )
        send.start()
        sends.append(send)

    cells, channels = frames.shape
    frame = cells // frame_count
    classes = lat_ref.shape[0]
    per = latent // classes
    for load in loads[2:5]:
        load.wait()
    x = frames[...]
    back = [x]
    for t in range(1, conv.shape[0]):
        back.append(jnp.concatenate(
            [jnp.zeros((t * frame, channels), BF16), frames[: cells - t * frame, :]], axis=0
        ))
    x = jnp.concatenate(back, axis=1)
    narrow = lat_ref[...]
    spread = jnp.concatenate([narrow] * (LANES // classes), axis=0)
    chunk = 256
    for n in range(channels // chunk):
        part = slice(n * chunk, (n + 1) * chunk)
        taps = jnp.concatenate([conv[t, :, part] for t in range(conv.shape[0])], axis=0)
        value = dot(x, taps)
        active = (value * jax.nn.sigmoid(value)).astype(BF16)
        partial = dot_nt(active, spread[:, part])
        if n == 0:
            wide[...] = partial
        else:
            wide[...] += partial
    for load in loads[5:]:
        load.wait()
    gram = dot_nt(embed[...], embed[...]) * (1.0 / depth)
    patches = jnp.zeros((row_count, LANES), F32)
    lane = iota((row_count, LANES), 1)
    for i in range(per):
        cell = wide[pl.ds(i, row_count, stride=per), :].astype(BF16).astype(F32)
        patches = jnp.where(lane // classes == i, cell, patches)
    slim = patches[:, :latent]
    exact = slim.astype(BF16)
    image = jnp.zeros((row_count, latent), F32)
    rest = gram
    for _ in range(3):
        piece = rest.astype(BF16)
        rest = rest - piece.astype(F32)
        image = image + dot(exact, piece)
    square = jnp.sum(slim * image, axis=1, keepdims=True)
    patches = patches * lax.rsqrt(jnp.maximum(square, 0.0) + EPS)
    joined = patches[:lines, :]
    for i in range(1, pack):
        joined = joined + pltpu.roll(patches[i * lines : (i + 1) * lines, :], i * latent, 1)
    packed[...] = joined.astype(BF16)

    for d in order:
        send = pltpu.make_async_remote_copy(
            src_ref=packed, dst_ref=rows_out.at[ctx],
            send_sem=row_send.at[d], recv_sem=row_recv.at[d],
            device_id=target(d), device_id_type=MESH,
        )
        send.start()
        sends.append(send)

    tile = 512
    for k in range(depth // tile):
        part = slice(k * tile, (k + 1) * tile)
        full = embed[:, part].astype(F32) * gain_ref[:, part]
        top = full.astype(BF16)
        scaled[:latent, part] = top
        scaled[latent:, part] = (full - top.astype(F32)).astype(BF16)

    def swap(j):
        return pltpu.make_async_remote_copy(
            src_ref=weff_out.at[section, j], dst_ref=weff_out.at[section, j],
            send_sem=half_send.at[j], recv_sem=half_recv.at[j],
            device_id={"section": other}, device_id_type=MESH,
        )

    def contract(j, carry):
        total[...] = jnp.zeros_like(total)

        def piece(p, inner):
            stream(j, p).wait()
            part = pl.ds(pl.multiple_of(p * step, step), step)
            total[...] += dot(scaled[:, part], qkv[j, part, :])
            return inner

        lax.fori_loop(0, pieces, piece, 0)
        full = total[...]
        weff_out[section, j] = (full[:latent] + full[latent:]).astype(BF16)
        swap(j).start()
        return carry

    lax.fori_loop(0, 3, contract, 0)
    for send in sends:
        send.wait()
    for j in range(3):
        swap(j).wait()


def attend_kernel(shards, capacity, rows_ref, meta_ref, weff_ref, out_hbm, out_ref, sem):
    ctx = lax.axis_index("ctx")
    sections, _, latent, half = weff_ref.shape
    lines = rows_ref.shape[1]
    pack = LANES // latent
    slots = out_ref.shape[0]
    blocks, labels, spots = [], [], []
    for source in range(shards):
        meta = meta_ref[source].astype(F32)
        labels.append(meta[2:3, :])
        home = meta[1:2, :] + (source * capacity)
        spots.append(jnp.where(meta[0:1, :] == ctx.astype(F32), home, -1.0))
        both = rows_ref[source]
        for i in range(pack):
            blocks.append(both[:, i * latent : (i + 1) * latent])
    rows = jnp.concatenate(blocks, axis=0)
    label = jnp.concatenate(labels, axis=1)
    spot = jnp.concatenate(spots, axis=1).astype(jnp.int32)
    taken = spot == iota((slots, spot.shape[1]), 0)
    picked = dot(taken.astype(F32).astype(BF16), rows).astype(BF16)
    own = jnp.sum(jnp.where(taken, label, 0.0), axis=1, keepdims=True)
    bias = jnp.where(label == own, 0.0, -1e30)

    def head_norm(x, factor):
        return x * (lax.rsqrt(jnp.mean(x * x, axis=-1, keepdims=True) + EPS) * factor)

    copies = []
    group = min(2, half // HEAD)
    pair = group * HEAD
    for i in range(sections):
        for g in range(half // pair):
            cols = slice(g * pair, (g + 1) * pair)
            q = dot(picked, weff_ref[i, 0, :, cols])
            k = dot(rows, weff_ref[i, 1, :, cols])
            v = dot(rows, weff_ref[i, 2, :, cols]).astype(BF16)
            for h in range(group):
                part = slice(h * HEAD, (h + 1) * HEAD)
                queries = head_norm(q[:, part], 1.0 / HEAD**0.5).astype(BF16)
                keys = head_norm(k[:, part], 1.0).astype(BF16)
                expo = jnp.exp(dot_nt(queries, keys) + bias)
                den = jnp.sum(expo, axis=1, keepdims=True)
                summed = dot(expo.astype(BF16), v[:, part])
                where = slice(i * half + g * pair + h * HEAD, i * half + g * pair + (h + 1) * HEAD)
                out_ref[:, where] = (summed * (1.0 / jnp.where(den > 0.0, den, 1.0))).astype(BF16)
            where = pl.ds(i * half + g * pair, pair)
            copy = pltpu.make_async_copy(out_ref.at[:, where], out_hbm.at[:, where], sem.at[len(copies)])
            copy.start()
            copies.append(copy)
    for copy in copies:
        copy.wait()


def on_device(shards, sections, frames, w_conv, w_lat, dest, pick, w_embed, gain, w_qkv):
    _, frame_count, frame, channels = frames.shape
    latent, depth = w_embed.shape
    cells = frame_count * frame
    row_count = dest.shape[1]
    columns = w_qkv.shape[2]
    half = columns // sections
    pieces = 4
    capacity = max(2, 3 * row_count // (2 * shards))
    slots = shards * capacity
    lines = row_count * latent // LANES
    rows, meta, weff = pl.pallas_call(
        functools.partial(encode_kernel, shards, frame_count, pieces),
        out_shape=(
            pltpu.VMEM((shards, lines, LANES), BF16),
            pltpu.VMEM((shards, META, row_count), BF16),
            pltpu.VMEM((sections, 3, latent, half), BF16),
        ),
        in_specs=[HBM] * 8,
        out_specs=(VMEM, VMEM, VMEM),
        scratch_shapes=[
            pltpu.VMEM((cells, channels), BF16),
            pltpu.VMEM(w_conv.shape, BF16),
            pltpu.VMEM((w_lat.shape[1], channels), BF16),
            pltpu.VMEM((sections, 1, row_count), jnp.int32),
            pltpu.VMEM((sections, row_count), jnp.int32),
            pltpu.VMEM((latent, depth), BF16),
            pltpu.VMEM((1, depth), F32),
            pltpu.VMEM((3, depth, half), BF16),
            pltpu.VMEM((2 * latent, depth), BF16),
            pltpu.VMEM((cells, LANES), F32),
            pltpu.VMEM((lines, LANES), BF16),
            pltpu.VMEM((META, row_count), BF16),
            pltpu.VMEM((2 * latent, half), F32),
            pltpu.SemaphoreType.DMA((7,)),
            pltpu.SemaphoreType.DMA((3 * pieces,)),
            pltpu.SemaphoreType.DMA((shards,)),
            pltpu.SemaphoreType.DMA((shards,)),
            pltpu.SemaphoreType.DMA((shards,)),
            pltpu.SemaphoreType.DMA((shards,)),
            pltpu.SemaphoreType.DMA((3,)),
            pltpu.SemaphoreType.DMA((3,)),
        ],
        compiler_params=pltpu.CompilerParams(
            collective_id=0, has_side_effects=True, vmem_limit_bytes=LIMIT
        ),
    )(
        frames.reshape(cells, channels),
        w_conv,
        w_lat.T,
        dest.transpose(0, 2, 1),
        pick,
        w_embed,
        gain.reshape(1, depth),
        w_qkv.transpose(1, 0, 2),
    )
    out = pl.pallas_call(
        functools.partial(attend_kernel, shards, capacity),
        out_shape=jax.ShapeDtypeStruct((slots, columns), BF16),
        in_specs=[VMEM, VMEM, VMEM],
        out_specs=HBM,
        scratch_shapes=[
            pltpu.VMEM((slots, columns), BF16),
            pltpu.SemaphoreType.DMA((columns // HEAD,)),
        ],
        compiler_params=pltpu.CompilerParams(vmem_limit_bytes=LIMIT // 2),
    )(rows, meta, weff)
    return out.reshape(1, slots, columns)


def solution(mesh):
    in_specs = (
        P("section", "ctx", None, None),
        P(),
        P(),
        P(None, "ctx", None),
        P(None, "ctx"),
        P(),
        P(),
        P(None, None, "mp"),
    )
    return jax.shard_map(
        functools.partial(on_device, mesh.shape["ctx"], mesh.shape["section"]),
        mesh=mesh,
        in_specs=in_specs,
        out_specs=P("section", "ctx", "mp"),
        check_vma=False,
    )
```

time: 17.9 us -> 19.4 us (1.084)
  Pallas kernels: 17.7 us -> 19.2 us
    pallas_call x1, Pallas kernels: 12.4 us -> 15.3 us  [on_device(): pl.pallas_call(functools.partial(encode_kernel, shards, frame_count, piec...]
    pallas_call x1, Pallas kernels: 5.33 us -> 3.9 us  [on_device(): pl.pallas_call(functools.partial(attend_kernel, shards, capacity), out_sh...]
where the time goes in v1:
time: 19.4 us; the launch traced here: 19.2 us
  Pallas kernels  19.2 us (99%)
    pallas_call x1, Pallas kernels, on_device(): pl.pallas_call(functools.partial(encode_kernel, shards, frame_count, piec...  15.3 us
    pallas_call x1, Pallas kernels, on_device(): pl.pallas_call(functools.partial(attend_kernel, shards, capacity), out_sh...  3.9 us

profile of v1, /device:TPU:1, one launch (start us, length us, event | category | flops | bytes accessed | tf_op | source)
XLA Modules:
  0.0 19.2 jit_solution(60325280676087193)
XLA Ops:
  0.0 15.3 %shard_map.82 = (bf16[4,64,128]{2,1,0:T(8,128)(2,1)S(1)}, bf16[4,16,128]{2,1,0:T(8,128)(2,1)S(1)}, bf16[2,3,64,512]{3,2,1,0:T(8,128)(2,1)S(1)}) custom-call(bf16[512,512]{1,0:T(8,128)(2,1)} %bitcast.7, bf16[3,512,512]{2,1,0:T(8,128)(2,1)} %conv_hbm.1, bf16[16,512]{1,0:T(8,128)(2,1)} %bitcast.9, s32[2,1,128]{2,1,0:T(1,128)} %bitcast.10, s32[2,128]{1,0:T(2,128)} %pick_hbm.1, ...), custom_call_target="tpu_custom_call" | custom-call | tf_op jit(solution)/shard_map/pallas_call | solution.py:271
  15.3 3.9 %shard_map.83 = bf16[192,1024]{1,0:T(8,128)(2,1)} custom-call(bf16[4,64,128]{2,1,0:T(8,128)(2,1)S(1)} %get-tuple-element.8.rows_ref, bf16[4,16,128]{2,1,0:T(8,128)(2,1)S(1)} %get-tuple-element.9.meta_ref, bf16[2,3,64,512]{3,2,1,0:T(8,128)(2,1)S(1)} %get-tuple-element.10.weff_ref), custom_call_target="tpu_custom_call" | custom-call | tf_op jit(solution)/shard_map/pallas_call | solution.py:316

commit v2 on v1

--- a/solution.py
+++ b/solution.py
@@ -59,8 +59,8 @@
     loads = [
         pltpu.make_async_copy(source, target, in_sem.at[i])
         for i, (source, target) in enumerate((
-            (dest_hbm, dest_ref), (pick_hbm, pick_ref), (lat_hbm, lat_ref),
-            (frames_hbm, frames), (conv_hbm, conv), (embed_hbm, embed), (gain_hbm, gain_ref),
+            (dest_hbm, dest_ref), (pick_hbm, pick_ref), (lat_hbm, lat_ref), (gain_hbm, gain_ref),
+            (embed_hbm, embed), (frames_hbm, frames), (conv_hbm, conv),
         ))
     ]
     for load in loads:
@@ -72,10 +72,6 @@
         return pltpu.make_async_copy(
             qkv_hbm.at[j, part, columns], qkv.at[j, part, :], qkv_sem.at[j * pieces + p]
         )
-
-    for j in range(3):
-        for p in range(pieces):
-            stream(j, p).start()
 
     def target(d):
         return {"section": other, "ctx": lax.rem(ctx + d, shards)}
@@ -99,23 +95,30 @@
     meta = jnp.where(line == 1, within, meta)
     meta = jnp.where(line == 2, label.astype(F32), meta)
     meta_ref[...] = meta.astype(BF16)
-    pl.semaphore_wait(barrier, shards)
-    sends = []
-    for d in order:
-        send = pltpu.make_async_remote_copy(
-            src_ref=meta_ref, dst_ref=meta_out.at[ctx],
-            send_sem=meta_send.at[d], recv_sem=meta_recv.at[d],
-            device_id=target(d), device_id_type=MESH,
-        )
-        send.start()
-        sends.append(send)
-
     cells, channels = frames.shape
     frame = cells // frame_count
     classes = lat_ref.shape[0]
     per = latent // classes
     for load in loads[2:5]:
         load.wait()
+    for j in range(1):
+        for p in range(pieces):
+            stream(j, p).start()
+
+    tile = 512
+    for k in range(depth // tile):
+        part = slice(k * tile, (k + 1) * tile)
+        full = embed[:, part].astype(F32) * gain_ref[:, part]
+        top = full.astype(BF16)
+        scaled[:latent, part] = top
+        scaled[latent:, part] = (full - top.astype(F32)).astype(BF16)
+    gram = dot_nt(embed[...], embed[...]) * (1.0 / depth)
+    for load in loads[5:]:
+        load.wait()
+    for j in range(1, 3):
+        for p in range(pieces):
+            stream(j, p).start()
+
     x = frames[...]
     back = [x]
     for t in range(1, conv.shape[0]):
@@ -130,15 +133,13 @@
         part = slice(n * chunk, (n + 1) * chunk)
         taps = jnp.concatenate([conv[t, :, part] for t in range(conv.shape[0])], axis=0)
         value = dot(x, taps)
-        active = (value * jax.nn.sigmoid(value)).astype(BF16)
+        value = 0.5 * value
+        active = (value * jnp.tanh(value) + value).astype(BF16)
         partial = dot_nt(active, spread[:, part])
         if n == 0:
             wide[...] = partial
         else:
             wide[...] += partial
-    for load in loads[5:]:
-        load.wait()
-    gram = dot_nt(embed[...], embed[...]) * (1.0 / depth)
     patches = jnp.zeros((row_count, LANES), F32)
     lane = iota((row_count, LANES), 1)
     for i in range(per):
@@ -159,23 +160,6 @@
         joined = joined + pltpu.roll(patches[i * lines : (i + 1) * lines, :], i * latent, 1)
     packed[...] = joined.astype(BF16)
 
-    for d in order:
-        send = pltpu.make_async_remote_copy(
-            src_ref=packed, dst_ref=rows_out.at[ctx],
-            send_sem=row_send.at[d], recv_sem=row_recv.at[d],
-            device_id=target(d), device_id_type=MESH,
-        )
-        send.start()
-        sends.append(send)
-
-    tile = 512
-    for k in range(depth // tile):
-        part = slice(k * tile, (k + 1) * tile)
-        full = embed[:, part].astype(F32) * gain_ref[:, part]
-        top = full.astype(BF16)
-        scaled[:latent, part] = top
-        scaled[latent:, part] = (full - top.astype(F32)).astype(BF16)
-
     def swap(j):
         return pltpu.make_async_remote_copy(
             src_ref=weff_out.at[section, j], dst_ref=weff_out.at[section, j],
@@ -183,7 +167,21 @@
             device_id={"section": other}, device_id_type=MESH,
         )
 
-    def contract(j, carry):
+    def post(d):
+        return pltpu.make_async_remote_copy(
+            src_ref=packed, dst_ref=rows_out.at[ctx],
+            send_sem=row_send.at[d], recv_sem=row_recv.at[d],
+            device_id=target(d), device_id_type=MESH,
+        )
+
+    def post_meta(d):
+        return pltpu.make_async_remote_copy(
+            src_ref=meta_ref, dst_ref=meta_out.at[ctx],
+            send_sem=meta_send.at[d], recv_sem=meta_recv.at[d],
+            device_id=target(d), device_id_type=MESH,
+        )
+
+    def contract(j):
         total[...] = jnp.zeros_like(total)
 
         def piece(p, inner):
@@ -195,12 +193,34 @@
         lax.fori_loop(0, pieces, piece, 0)
         full = total[...]
         weff_out[section, j] = (full[:latent] + full[latent:]).astype(BF16)
+
+    early = ctx == 0
+
+    @pl.when(early)
+    def _():
+        contract(0)
+
+    pl.semaphore_wait(barrier, shards)
+    for d in order:
+        post(d).start()
+    for d in order:
+        post_meta(d).start()
+
+    @pl.when(jnp.logical_not(early))
+    def _():
+        contract(0)
+
+    swap(0).start()
+
+    def later(j, carry):
+        contract(j)
         swap(j).start()
         return carry
 
-    lax.fori_loop(0, 3, contract, 0)
-    for send in sends:
-        send.wait()
+    lax.fori_loop(1, 3, later, 0)
+    for d in order:
+        post(d).wait()
+        post_meta(d).wait()
     for j in range(3):
         swap(j).wait()
 

time: 19.4 us -> 14.9 us (0.77)
  Pallas kernels: 19.2 us -> 14.7 us
    pallas_call x1, Pallas kernels: 15.3 us -> 10.8 us  [on_device(): pl.pallas_call(functools.partial(encode_kernel, shards, frame_count, piec...]
where the time goes in v2:
time: 14.9 us; the launch traced here: 14.7 us
  Pallas kernels  14.7 us (99%)
    pallas_call x1, Pallas kernels, on_device(): pl.pallas_call(functools.partial(encode_kernel, shards, frame_count, piec...  10.8 us
    pallas_call x1, Pallas kernels, on_device(): pl.pallas_call(functools.partial(attend_kernel, shards, capacity), out_sh...  3.9 us

profile of v2, /device:TPU:1, one launch (start us, length us, event | category | flops | bytes accessed | tf_op | source)
XLA Modules:
  0.0 14.7 jit_solution(6207631132479203878)
XLA Ops:
  0.0 10.8 %shard_map.82 = (bf16[4,64,128]{2,1,0:T(8,128)(2,1)S(1)}, bf16[4,16,128]{2,1,0:T(8,128)(2,1)S(1)}, bf16[2,3,64,512]{3,2,1,0:T(8,128)(2,1)S(1)}) custom-call(bf16[512,512]{1,0:T(8,128)(2,1)} %bitcast.7, bf16[3,512,512]{2,1,0:T(8,128)(2,1)} %conv_hbm.1, bf16[16,512]{1,0:T(8,128)(2,1)} %bitcast.9, s32[2,1,128]{2,1,0:T(1,128)} %bitcast.10, s32[2,128]{1,0:T(2,128)} %pick_hbm.1, ...), custom_call_target="tpu_custom_call" | custom-call | tf_op jit(solution)/shard_map/pallas_call | solution.py:291
  10.8 3.9 %shard_map.83 = bf16[192,1024]{1,0:T(8,128)(2,1)} custom-call(bf16[4,64,128]{2,1,0:T(8,128)(2,1)S(1)} %get-tuple-element.8.rows_ref, bf16[4,16,128]{2,1,0:T(8,128)(2,1)S(1)} %get-tuple-element.9.meta_ref, bf16[2,3,64,512]{3,2,1,0:T(8,128)(2,1)S(1)} %get-tuple-element.10.weff_ref), custom_call_target="tpu_custom_call" | custom-call | tf_op jit(solution)/shard_map/pallas_call | solution.py:336

commit v3 on v2

--- a/solution.py
+++ b/solution.py
@@ -17,7 +17,7 @@
 BF16 = jnp.bfloat16
 HBM = pl.BlockSpec(memory_space=pltpu.HBM)
 VMEM = pl.BlockSpec(memory_space=pltpu.VMEM)
-LIMIT = 60 * 1024 * 1024
+LIMIT = 40 * 1024 * 1024
 
 
 def dot(a, b):
@@ -35,9 +35,9 @@
 def encode_kernel(
     shards, frame_count, pieces,
     frames_hbm, conv_hbm, lat_hbm, dest_hbm, pick_hbm, embed_hbm, gain_hbm, qkv_hbm,
-    rows_out, meta_out, weff_out,
-    frames, conv, lat_ref, dest_ref, pick_ref, embed, gain_ref, qkv, scaled, wide, packed, meta_ref, total,
-    in_sem, qkv_sem, row_send, row_recv, meta_send, meta_recv, half_send, half_recv,
+    weff_out, rows_out, queries_out, keys_out, bias_out,
+    frames, conv, lat_ref, dest_ref, pick_ref, embed, gain_ref, qkv, scaled, wide, packed, inbox, total,
+    in_sem, qkv_sem, row_send, row_recv, half_send, half_recv,
 ):
     section = lax.axis_index("section")
     ctx = lax.axis_index("ctx")
@@ -50,6 +50,10 @@
     pack = LANES // latent
     lines = row_count // pack
 
+    cells, channels = frames.shape
+    chunks = 2
+    chunk = channels // chunks
+
     barrier = pltpu.get_barrier_semaphore()
     for d in range(shards):
         pl.semaphore_signal(
@@ -60,7 +64,10 @@
         pltpu.make_async_copy(source, target, in_sem.at[i])
         for i, (source, target) in enumerate((
             (dest_hbm, dest_ref), (pick_hbm, pick_ref), (lat_hbm, lat_ref), (gain_hbm, gain_ref),
-            (embed_hbm, embed), (frames_hbm, frames), (conv_hbm, conv),
+            (embed_hbm, embed), (frames_hbm, frames),
+        ) + tuple(
+            (conv_hbm.at[:, :, pl.ds(n * chunk, chunk)], conv.at[:, :, pl.ds(n * chunk, chunk)])
+            for n in range(chunks)
         ))
     ]
     for load in loads:
@@ -72,11 +79,6 @@
         return pltpu.make_async_copy(
             qkv_hbm.at[j, part, columns], qkv.at[j, part, :], qkv_sem.at[j * pieces + p]
         )
-
-    def target(d):
-        return {"section": other, "ctx": lax.rem(ctx + d, shards)}
-
-    order = sorted(range(shards), key=lambda d: -min(d, shards - d))
 
     loads[0].wait()
     loads[1].wait()
@@ -94,8 +96,7 @@
     meta = jnp.where(line == 0, dest.astype(F32), 0.0)
     meta = jnp.where(line == 1, within, meta)
     meta = jnp.where(line == 2, label.astype(F32), meta)
-    meta_ref[...] = meta.astype(BF16)
-    cells, channels = frames.shape
+    packed[lines:, :] = meta.astype(BF16)
     frame = cells // frame_count
     classes = lat_ref.shape[0]
     per = latent // classes
@@ -113,8 +114,7 @@
         scaled[:latent, part] = top
         scaled[latent:, part] = (full - top.astype(F32)).astype(BF16)
     gram = dot_nt(embed[...], embed[...]) * (1.0 / depth)
-    for load in loads[5:]:
-        load.wait()
+    loads[5].wait()
     for j in range(1, 3):
         for p in range(pieces):
             stream(j, p).start()
@@ -128,8 +128,8 @@
     x = jnp.concatenate(back, axis=1)
     narrow = lat_ref[...]
     spread = jnp.concatenate([narrow] * (LANES // classes), axis=0)
-    chunk = 256
-    for n in range(channels // chunk):
+    for n in range(chunks):
+        loads[6 + n].wait()
         part = slice(n * chunk, (n + 1) * chunk)
         taps = jnp.concatenate([conv[t, :, part] for t in range(conv.shape[0])], axis=0)
         value = dot(x, taps)
@@ -158,7 +158,7 @@
     joined = patches[:lines, :]
     for i in range(1, pack):
         joined = joined + pltpu.roll(patches[i * lines : (i + 1) * lines, :], i * latent, 1)
-    packed[...] = joined.astype(BF16)
+    packed[:lines, :] = joined.astype(BF16)
 
     def swap(j):
         return pltpu.make_async_remote_copy(
@@ -167,18 +167,16 @@
             device_id={"section": other}, device_id_type=MESH,
         )
 
-    def post(d):
+    def post(t):
         return pltpu.make_async_remote_copy(
-            src_ref=packed, dst_ref=rows_out.at[ctx],
-            send_sem=row_send.at[d], recv_sem=row_recv.at[d],
-            device_id=target(d), device_id_type=MESH,
-        )
-
-    def post_meta(d):
+            src_ref=packed, dst_ref=inbox.at[ctx], send_sem=row_send.at[t], recv_sem=row_recv.at[ctx],
+            device_id={"section": other, "ctx": t}, device_id_type=MESH,
+        )
+
+    def arrival(c):
         return pltpu.make_async_remote_copy(
-            src_ref=meta_ref, dst_ref=meta_out.at[ctx],
-            send_sem=meta_send.at[d], recv_sem=meta_recv.at[d],
-            device_id=target(d), device_id_type=MESH,
+            src_ref=packed, dst_ref=inbox.at[c], send_sem=row_send.at[c], recv_sem=row_recv.at[c],
+            device_id={"section": other, "ctx": c}, device_id_type=MESH,
         )
 
     def contract(j):
@@ -201,10 +199,8 @@
         contract(0)
 
     pl.semaphore_wait(barrier, shards)
-    for d in order:
-        post(d).start()
-    for d in order:
-        post_meta(d).start()
+    for t in range(shards):
+        post(t).start()
 
     @pl.when(jnp.logical_not(early))
     def _():
@@ -218,56 +214,61 @@
         return carry
 
     lax.fori_loop(1, 3, later, 0)
-    for d in order:
-        post(d).wait()
-        post_meta(d).wait()
-    for j in range(3):
-        swap(j).wait()
-
-
-def attend_kernel(shards, capacity, rows_ref, meta_ref, weff_ref, out_hbm, out_ref, sem):
-    ctx = lax.axis_index("ctx")
-    sections, _, latent, half = weff_ref.shape
-    lines = rows_ref.shape[1]
-    pack = LANES // latent
-    slots = out_ref.shape[0]
-    blocks, labels, spots = [], [], []
-    for source in range(shards):
-        meta = meta_ref[source].astype(F32)
+    sections = weff_out.shape[0]
+
+    def head_norm(x, factor):
+        return x * (lax.rsqrt(jnp.mean(x * x, axis=-1, keepdims=True) + EPS) * factor)
+
+    def project(x, j, out, first_row, factor):
+        count = x.shape[0]
+        for i in range(sections):
+            y = dot(x, weff_out[i, j])
+            for h in range(half // HEAD):
+                z = head_norm(y[:, h * HEAD : (h + 1) * HEAD], factor).astype(BF16)
+                out[first_row : first_row + count, i * half + h * HEAD : i * half + (h + 1) * HEAD] = z
+
+    swap(0).wait_recv()
+    swap(1).wait_recv()
+    capacity = queries_out.shape[0] // shards
+    slots = queries_out.shape[0]
+    labels, spots = [], []
+    for c in range(shards):
+        arrival(c).wait_recv()
+        both = inbox[c, :lines, :]
+        block = jnp.concatenate([both[:, i * latent : (i + 1) * latent] for i in range(pack)], axis=0)
+        rows_out[c * row_count : (c + 1) * row_count, :] = block
+        project(block, 1, keys_out, c * row_count, 1.0)
+        meta = inbox[c, lines:, :].astype(F32)
         labels.append(meta[2:3, :])
-        home = meta[1:2, :] + (source * capacity)
-        spots.append(jnp.where(meta[0:1, :] == ctx.astype(F32), home, -1.0))
-        both = rows_ref[source]
-        for i in range(pack):
-            blocks.append(both[:, i * latent : (i + 1) * latent])
-    rows = jnp.concatenate(blocks, axis=0)
+        spots.append(jnp.where(meta[0:1, :] == ctx.astype(F32), meta[1:2, :] + (c * capacity), -1.0))
     label = jnp.concatenate(labels, axis=1)
     spot = jnp.concatenate(spots, axis=1).astype(jnp.int32)
     taken = spot == iota((slots, spot.shape[1]), 0)
-    picked = dot(taken.astype(F32).astype(BF16), rows).astype(BF16)
+    picked = dot(taken.astype(F32).astype(BF16), rows_out[...]).astype(BF16)
     own = jnp.sum(jnp.where(taken, label, 0.0), axis=1, keepdims=True)
-    bias = jnp.where(label == own, 0.0, -1e30)
-
-    def head_norm(x, factor):
-        return x * (lax.rsqrt(jnp.mean(x * x, axis=-1, keepdims=True) + EPS) * factor)
-
+    bias_out[...] = jnp.where(label == own, 0.0, -1e30)
+    project(picked, 0, queries_out, 0, 1.0 / HEAD**0.5)
+    for t in range(shards):
+        post(t).wait_send()
+    for j in range(3):
+        swap(j).wait_send()
+    swap(2).wait_recv()
+
+
+def attend_kernel(weff_ref, rows_ref, queries_ref, keys_ref, bias_ref, out_hbm, out_ref, sem):
+    sections, _, _, half = weff_ref.shape
+    rows = rows_ref[...]
     copies = []
     group = min(2, half // HEAD)
     pair = group * HEAD
     for i in range(sections):
         for g in range(half // pair):
-            cols = slice(g * pair, (g + 1) * pair)
-            q = dot(picked, weff_ref[i, 0, :, cols])
-            k = dot(rows, weff_ref[i, 1, :, cols])
-            v = dot(rows, weff_ref[i, 2, :, cols]).astype(BF16)
+            v = dot(rows, weff_ref[i, 2, :, g * pair : (g + 1) * pair]).astype(BF16)
             for h in range(group):
-                part = slice(h * HEAD, (h + 1) * HEAD)
-                queries = head_norm(q[:, part], 1.0 / HEAD**0.5).astype(BF16)
-                keys = head_norm(k[:, part], 1.0).astype(BF16)
-                expo = jnp.exp(dot_nt(queries, keys) + bias)
+                where = slice(i * half + g * pair + h * HEAD, i * half + g * pair + (h + 1) * HEAD)
+                expo = jnp.exp(dot_nt(queries_ref[:, where], keys_ref[:, where]) + bias_ref[...])
                 den = jnp.sum(expo, axis=1, keepdims=True)
-                summed = dot(expo.astype(BF16), v[:, part])
-                where = slice(i * half + g * pair + h * HEAD, i * half + g * pair + (h + 1) * HEAD)
+                summed = dot(expo.astype(BF16), v[:, h * HEAD : (h + 1) * HEAD])
                 out_ref[:, where] = (summed * (1.0 / jnp.where(den > 0.0, den, 1.0))).astype(BF16)
             where = pl.ds(i * half + g * pair, pair)
             copy = pltpu.make_async_copy(out_ref.at[:, where], out_hbm.at[:, where], sem.at[len(copies)])
@@ -288,15 +289,18 @@
     capacity = max(2, 3 * row_count // (2 * shards))
     slots = shards * capacity
     lines = row_count * latent // LANES
-    rows, meta, weff = pl.pallas_call(
+    total_rows = shards * row_count
+    handed = pl.pallas_call(
         functools.partial(encode_kernel, shards, frame_count, pieces),
         out_shape=(
-            pltpu.VMEM((shards, lines, LANES), BF16),
-            pltpu.VMEM((shards, META, row_count), BF16),
             pltpu.VMEM((sections, 3, latent, half), BF16),
+            pltpu.VMEM((total_rows, latent), BF16),
+            pltpu.VMEM((slots, columns), BF16),
+            pltpu.VMEM((total_rows, columns), BF16),
+            pltpu.VMEM((slots, total_rows), F32),
         ),
         in_specs=[HBM] * 8,
-        out_specs=(VMEM, VMEM, VMEM),
+        out_specs=(VMEM,) * 5,
         scratch_shapes=[
             pltpu.VMEM((cells, channels), BF16),
             pltpu.VMEM(w_conv.shape, BF16),
@@ -308,13 +312,11 @@
             pltpu.VMEM((3, depth, half), BF16),
             pltpu.VMEM((2 * latent, depth), BF16),
             pltpu.VMEM((cells, LANES), F32),
-            pltpu.VMEM((lines, LANES), BF16),
-            pltpu.VMEM((META, row_count), BF16),
+            pltpu.VMEM((lines + META, LANES), BF16),
+            pltpu.VMEM((shards, lines + META, LANES), BF16),
             pltpu.VMEM((2 * latent, half), F32),
-            pltpu.SemaphoreType.DMA((7,)),
+            pltpu.SemaphoreType.DMA((8,)),
             pltpu.SemaphoreType.DMA((3 * pieces,)),
-            pltpu.SemaphoreType.DMA((shards,)),
-            pltpu.SemaphoreType.DMA((shards,)),
             pltpu.SemaphoreType.DMA((shards,)),
             pltpu.SemaphoreType.DMA((shards,)),
             pltpu.SemaphoreType.DMA((3,)),
@@ -334,16 +336,16 @@
         w_qkv.transpose(1, 0, 2),
     )
     out = pl.pallas_call(
-        functools.partial(attend_kernel, shards, capacity),
+        attend_kernel,
         out_shape=jax.ShapeDtypeStruct((slots, columns), BF16),
-        in_specs=[VMEM, VMEM, VMEM],
+        in_specs=[VMEM] * 5,
         out_specs=HBM,
         scratch_shapes=[
             pltpu.VMEM((slots, columns), BF16),
             pltpu.SemaphoreType.DMA((columns // HEAD,)),
         ],
         compiler_params=pltpu.CompilerParams(vmem_limit_bytes=LIMIT // 2),
-    )(rows, meta, weff)
+    )(*handed)
     return out.reshape(1, slots, columns)
 
 

time: 14.9 us -> 20.2 us (1.36)
  local copies, waits for them, and re-layouts: 0 us -> 6.39 us
  Pallas kernels: 14.7 us -> 13.5 us
    unnamed x0 -> x14, local copies, waits for them, and re-layouts: none -> 6.39 us
    pallas_call x1, Pallas kernels: 3.9 us -> 2.64 us  [on_device(): pl.pallas_call(attend_kernel, out_shape=jax.ShapeDtypeStruct((slots, colu...]
where the time goes in v3:
time: 20.2 us; the launch traced here: 19.9 us
  Pallas kernels  13.5 us (67%)
  local copies, waits for them, and re-layouts  6.39 us (32%)
    pallas_call x1, Pallas kernels, on_device(): pl.pallas_call(functools.partial(encode_kernel, shards, frame_count, piec...  10.8 us
    unnamed x14, local copies, waits for them, and re-layouts  6.39 us
    pallas_call x1, Pallas kernels, on_device(): pl.pallas_call(attend_kernel, out_shape=jax.ShapeDtypeStruct((slots, colu...  2.64 us

profile of v3, /device:TPU:1, one launch (start us, length us, event | category | flops | bytes accessed | tf_op | source)
XLA Modules:
  0.0 19.9 jit_solution(15184943833916263457)
XLA Ops:
  0.0 0.0 copy-start
  0.0 1.4 %copy-done = bf16[3,512,512]{2,1,0:T(8,128)(2,1)S(1)} copy-done((bf16[3,512,512]{2,1,0:T(8,128)(2,1)S(1)}, bf16[3,512,512]{2,1,0:T(8,128)(2,1)}, u32[]{:S(2)}) %copy-start) | copy-done | bytes 1572888
  1.4 0.0 copy-start.1
  1.4 1.1 %copy-done.1 = bf16[64,6144]{1,0:T(8,128)(2,1)S(1)} copy-done((bf16[64,6144]{1,0:T(8,128)(2,1)S(1)}, bf16[64,6144]{1,0:T(8,128)(2,1)}, u32[]{:S(2)}) %copy-start.1) | copy-done | bytes 786456
  2.5 0.0 copy-start.2
  2.5 1.0 %copy-done.2 = bf16[1,4,128,512]{3,2,1,0:T(8,128)(2,1)S(1)} copy-done((bf16[1,4,128,512]{3,2,1,0:T(8,128)(2,1)S(1)}, bf16[1,4,128,512]{3,2,1,0:T(8,128)(2,1)}, u32[]{:S(2)}) %copy-start.2) | copy-done | bytes 524312
  3.6 0.0 copy-start.3
  3.6 0.7 %copy-done.3 = f32[6144]{0:T(1024)S(1)} copy-done((f32[6144]{0:T(1024)S(1)}, f32[6144]{0:T(1024)}, u32[]{:S(2)}) %copy-start.3) | copy-done | bytes 24600
  4.3 0.0 copy-start.4
  4.3 0.7 %copy-done.4 = bf16[512,16]{0,1:T(8,128)(2,1)S(1)} copy-done((bf16[512,16]{0,1:T(8,128)(2,1)S(1)}, bf16[512,16]{0,1:T(8,128)(2,1)}, u32[]{:S(2)}) %copy-start.4) | copy-done | bytes 16408
  5.0 0.0 copy-start.5
  5.0 0.7 %copy-done.5 = s32[2,128,1]{1,2,0:T(1,128)S(1)} copy-done((s32[2,128,1]{1,2,0:T(1,128)S(1)}, s32[2,128,1]{1,2,0:T(1,128)}, u32[]{:S(2)}) %copy-start.5) | copy-done | bytes 1048
  5.7 0.0 copy-start.6
  5.7 0.7 %copy-done.6 = s32[2,128]{1,0:T(2,128)S(1)} copy-done((s32[2,128]{1,0:T(2,128)S(1)}, s32[2,128]{1,0:T(2,128)}, u32[]{:S(2)}) %copy-start.6) | copy-done | bytes 1048
  6.4 10.8 %shard_map.82 = (bf16[2,3,64,512]{3,2,1,0:T(8,128)(2,1)S(1)}, bf16[512,64]{1,0:T(8,128)(2,1)S(1)}, bf16[192,1024]{1,0:T(8,128)(2,1)S(1)}, bf16[512,1024]{1,0:T(8,128)(2,1)S(1)}, f32[192,512]{1,0:T(8,128)S(1)}) custom-call(bf16[512,512]{1,0:T(8,128)(2,1)S(1)} %bitcast.6, bf16[3,512,512]{2,1,0:T(8,128)(2,1)S(1)} %copy-done, bf16[16,512]{1,0:T(8,128)(2,1)S(1)} %bitcast.8, ...), custom_call_target="tpu_custom_call" | custom-call | tf_op jit(solution)/shard_map/pallas_call | solution.py:293
  17.2 2.6 %shard_map.83 = bf16[192,1024]{1,0:T(8,128)(2,1)} custom-call(bf16[2,3,64,512]{3,2,1,0:T(8,128)(2,1)S(1)} %get-tuple-element.10.weff_ref, bf16[512,64]{1,0:T(8,128)(2,1)S(1)} %get-tuple-element.11.rows_ref, bf16[192,1024]{1,0:T(8,128)(2,1)S(1)} %get-tuple-element.12.queries_ref, bf16[512,1024]{1,0:T(8,128)(2,1)S(1)} %get-tuple-element.13.keys_ref, ...), custom_call_target="tpu_custom_call" | custom-call | tf_op jit(solution)/shard_map/pallas_call | solution.py:338
Async XLA Ops:
  0.0 1.4 %copy-start = (bf16[3,512,512]{2,1,0:T(8,128)(2,1)S(1)}, bf16[3,512,512]{2,1,0:T(8,128)(2,1)}, u32[]{:S(2)}) copy-start(bf16[3,512,512]{2,1,0:T(8,128)(2,1)} %conv_hbm.1) | copy-start | bytes 4718596
  1.4 1.1 %copy-start.1 = (bf16[64,6144]{1,0:T(8,128)(2,1)S(1)}, bf16[64,6144]{1,0:T(8,128)(2,1)}, u32[]{:S(2)}) copy-start(bf16[64,6144]{1,0:T(8,128)(2,1)} %embed_hbm.1) | copy-start | bytes 2359300
  2.5 1.0 %copy-start.2 = (bf16[1,4,128,512]{3,2,1,0:T(8,128)(2,1)S(1)}, bf16[1,4,128,512]{3,2,1,0:T(8,128)(2,1)}, u32[]{:S(2)}) copy-start(bf16[1,4,128,512]{3,2,1,0:T(8,128)(2,1)} %param.8) | copy-start | bytes 1572868
  3.6 0.7 %copy-start.3 = (f32[6144]{0:T(1024)S(1)}, f32[6144]{0:T(1024)}, u32[]{:S(2)}) copy-start(f32[6144]{0:T(1024)} %param.14) | copy-start | bytes 73732
  4.3 0.7 %copy-start.4 = (bf16[512,16]{0,1:T(8,128)(2,1)S(1)}, bf16[512,16]{0,1:T(8,128)(2,1)}, u32[]{:S(2)}) copy-start(bf16[512,16]{0,1:T(8,128)(2,1)} %param.10) | copy-start | bytes 49156
  5.0 0.7 %copy-start.5 = (s32[2,128,1]{1,2,0:T(1,128)S(1)}, s32[2,128,1]{1,2,0:T(1,128)}, u32[]{:S(2)}) copy-start(s32[2,128,1]{1,2,0:T(1,128)} %param.11) | copy-start | bytes 3076
  5.7 0.7 %copy-start.6 = (s32[2,128]{1,0:T(2,128)S(1)}, s32[2,128]{1,0:T(2,128)}, u32[]{:S(2)}) copy-start(s32[2,128]{1,0:T(2,128)} %pick_hbm.1) | copy-start | bytes 3076

commit v4 on v3

--- a/solution.py
+++ b/solution.py
@@ -17,7 +17,7 @@
 BF16 = jnp.bfloat16
 HBM = pl.BlockSpec(memory_space=pltpu.HBM)
 VMEM = pl.BlockSpec(memory_space=pltpu.VMEM)
-LIMIT = 40 * 1024 * 1024
+LIMIT = 56 * 1024 * 1024
 
 
 def dot(a, b):

time: 20.2 us -> 14.4 us (0.71); the launches traced: 19.9 us -> 14.3 us
  local copies, waits for them, and re-layouts: 6.39 us -> 0 us
  Pallas kernels: 13.5 us -> 14.3 us
    unnamed x14 -> x0, local copies, waits for them, and re-layouts: 6.39 us -> none
    pallas_call x1, Pallas kernels: 10.8 us -> 11.6 us  [on_device(): pl.pallas_call(functools.partial(encode_kernel, shards, frame_count, piec...]
where the time goes in v4:
time: 14.4 us; the launch traced here: 14.3 us
  Pallas kernels  14.3 us (99%)
    pallas_call x1, Pallas kernels, on_device(): pl.pallas_call(functools.partial(encode_kernel, shards, frame_count, piec...  11.6 us
    pallas_call x1, Pallas kernels, on_device(): pl.pallas_call(attend_kernel, out_shape=jax.ShapeDtypeStruct((slots, colu...  2.64 us

profile of v4, /device:TPU:1, one launch (start us, length us, event | category | flops | bytes accessed | tf_op | source)
XLA Modules:
  0.0 14.3 jit_solution(386760077943354462)
XLA Ops:
  0.0 11.6 %shard_map.82 = (bf16[2,3,64,512]{3,2,1,0:T(8,128)(2,1)S(1)}, bf16[512,64]{1,0:T(8,128)(2,1)S(1)}, bf16[192,1024]{1,0:T(8,128)(2,1)S(1)}, bf16[512,1024]{1,0:T(8,128)(2,1)S(1)}, f32[192,512]{1,0:T(8,128)S(1)}) custom-call(bf16[512,512]{1,0:T(8,128)(2,1)} %bitcast.7, bf16[3,512,512]{2,1,0:T(8,128)(2,1)} %conv_hbm.1, bf16[16,512]{1,0:T(8,128)(2,1)} %bitcast.9, ...), custom_call_target="tpu_custom_call" | custom-call | tf_op jit(solution)/shard_map/pallas_call | solution.py:293
  11.6 2.6 %shard_map.83 = bf16[192,1024]{1,0:T(8,128)(2,1)} custom-call(bf16[2,3,64,512]{3,2,1,0:T(8,128)(2,1)S(1)} %get-tuple-element.10.weff_ref, bf16[512,64]{1,0:T(8,128)(2,1)S(1)} %get-tuple-element.11.rows_ref, bf16[192,1024]{1,0:T(8,128)(2,1)S(1)} %get-tuple-element.12.queries_ref, bf16[512,1024]{1,0:T(8,128)(2,1)S(1)} %get-tuple-element.13.keys_ref, ...), custom_call_target="tpu_custom_call" | custom-call | tf_op jit(solution)/shard_map/pallas_call | solution.py:338

commit v5 on v4

--- a/solution.py
+++ b/solution.py
@@ -107,12 +107,6 @@
             stream(j, p).start()
 
     tile = 512
-    for k in range(depth // tile):
-        part = slice(k * tile, (k + 1) * tile)
-        full = embed[:, part].astype(F32) * gain_ref[:, part]
-        top = full.astype(BF16)
-        scaled[:latent, part] = top
-        scaled[latent:, part] = (full - top.astype(F32)).astype(BF16)
     gram = dot_nt(embed[...], embed[...]) * (1.0 / depth)
     loads[5].wait()
     for j in range(1, 3):
@@ -129,7 +123,9 @@
     narrow = lat_ref[...]
     spread = jnp.concatenate([narrow] * (LANES // classes), axis=0)
     for n in range(chunks):
-        loads[6 + n].wait()
+        if n == 0:
+            loads[6].wait()
+            loads[7].wait()
         part = slice(n * chunk, (n + 1) * chunk)
         taps = jnp.concatenate([conv[t, :, part] for t in range(conv.shape[0])], axis=0)
         value = dot(x, taps)
@@ -189,13 +185,18 @@
             return inner
 
         lax.fori_loop(0, pieces, piece, 0)
-        full = total[...]
-        weff_out[section, j] = (full[:latent] + full[latent:]).astype(BF16)
+        weff_out[section, j] = total[...].astype(BF16)
 
     early = ctx == 0
+
+    def scale_embed():
+        for k in range(depth // tile):
+            part = slice(k * tile, (k + 1) * tile)
+            scaled[:, part] = (embed[:, part].astype(F32) * gain_ref[:, part]).astype(BF16)
 
     @pl.when(early)
     def _():
+        scale_embed()
         contract(0)
 
     pl.semaphore_wait(barrier, shards)
@@ -204,6 +205,7 @@
 
     @pl.when(jnp.logical_not(early))
     def _():
+        scale_embed()
         contract(0)
 
     swap(0).start()
@@ -216,16 +218,18 @@
     lax.fori_loop(1, 3, later, 0)
     sections = weff_out.shape[0]
 
-    def head_norm(x, factor):
-        return x * (lax.rsqrt(jnp.mean(x * x, axis=-1, keepdims=True) + EPS) * factor)
+    pair = min(2 * HEAD, half)
+    same_head = iota((pair, pair), 0) // HEAD == iota((pair, pair), 1) // HEAD
+    average = jnp.where(same_head, 1.0 / HEAD, 0.0).astype(BF16)
 
     def project(x, j, out, first_row, factor):
         count = x.shape[0]
         for i in range(sections):
-            y = dot(x, weff_out[i, j])
-            for h in range(half // HEAD):
-                z = head_norm(y[:, h * HEAD : (h + 1) * HEAD], factor).astype(BF16)
-                out[first_row : first_row + count, i * half + h * HEAD : i * half + (h + 1) * HEAD] = z
+            for g in range(half // pair):
+                y = dot(x, weff_out[i, j, :, g * pair : (g + 1) * pair])
+                mean = dot((y * y).astype(BF16), average)
+                z = (y * (lax.rsqrt(mean + EPS) * factor)).astype(BF16)
+                out[first_row : first_row + count, i * half + g * pair : i * half + (g + 1) * pair] = z
 
     swap(0).wait_recv()
     swap(1).wait_recv()
@@ -285,7 +289,7 @@
     row_count = dest.shape[1]
     columns = w_qkv.shape[2]
     half = columns // sections
-    pieces = 4
+    pieces = 2
     capacity = max(2, 3 * row_count // (2 * shards))
     slots = shards * capacity
     lines = row_count * latent // LANES
@@ -310,11 +314,11 @@
             pltpu.VMEM((latent, depth), BF16),
             pltpu.VMEM((1, depth), F32),
             pltpu.VMEM((3, depth, half), BF16),
-            pltpu.VMEM((2 * latent, depth), BF16),
+            pltpu.VMEM((latent, depth), BF16),
             pltpu.VMEM((cells, LANES), F32),
             pltpu.VMEM((lines + META, LANES), BF16),
             pltpu.VMEM((shards, lines + META, LANES), BF16),
-            pltpu.VMEM((2 * latent, half), F32),
+            pltpu.VMEM((latent, half), F32),
             pltpu.SemaphoreType.DMA((8,)),
             pltpu.SemaphoreType.DMA((3 * pieces,)),
             pltpu.SemaphoreType.DMA((shards,)),

time: 14.4 us -> 13.8 us (0.958)
  Pallas kernels: 14.3 us -> 13.6 us
    pallas_call x1, Pallas kernels: 11.6 us -> 11 us  [on_device(): pl.pallas_call(functools.partial(encode_kernel, shards, frame_count, piec...]
where the time goes in v5:
time: 13.8 us; the launch traced here: 13.6 us
  Pallas kernels  13.6 us (99%)
    pallas_call x1, Pallas kernels, on_device(): pl.pallas_call(functools.partial(encode_kernel, shards, frame_count, piec...  11 us
    pallas_call x1, Pallas kernels, on_device(): pl.pallas_call(attend_kernel, out_shape=jax.ShapeDtypeStruct((slots, colu...  2.64 us

profile of v5, /device:TPU:1, one launch (start us, length us, event | category | flops | bytes accessed | tf_op | source)
XLA Modules:
  0.0 13.6 jit_solution(6948892524951670690)
XLA Ops:
  0.0 11.0 %shard_map.82 = (bf16[2,3,64,512]{3,2,1,0:T(8,128)(2,1)S(1)}, bf16[512,64]{1,0:T(8,128)(2,1)S(1)}, bf16[192,1024]{1,0:T(8,128)(2,1)S(1)}, bf16[512,1024]{1,0:T(8,128)(2,1)S(1)}, f32[192,512]{1,0:T(8,128)S(1)}) custom-call(bf16[512,512]{1,0:T(8,128)(2,1)} %bitcast.7, bf16[3,512,512]{2,1,0:T(8,128)(2,1)} %conv_hbm.1, bf16[16,512]{1,0:T(8,128)(2,1)} %bitcast.9, ...), custom_call_target="tpu_custom_call" | custom-call | tf_op jit(solution)/shard_map/pallas_call | solution.py:297
  11.0 2.6 %shard_map.83 = bf16[192,1024]{1,0:T(8,128)(2,1)} custom-call(bf16[2,3,64,512]{3,2,1,0:T(8,128)(2,1)S(1)} %get-tuple-element.10.weff_ref, bf16[512,64]{1,0:T(8,128)(2,1)S(1)} %get-tuple-element.11.rows_ref, bf16[192,1024]{1,0:T(8,128)(2,1)S(1)} %get-tuple-element.12.queries_ref, bf16[512,1024]{1,0:T(8,128)(2,1)S(1)} %get-tuple-element.13.keys_ref, ...), custom_call_target="tpu_custom_call" | custom-call | tf_op jit(solution)/shard_map/pallas_call | solution.py:342

commit v6 on v5

--- a/solution.py
+++ b/solution.py
@@ -236,15 +236,20 @@
     capacity = queries_out.shape[0] // shards
     slots = queries_out.shape[0]
     labels, spots = [], []
-    for c in range(shards):
-        arrival(c).wait_recv()
-        both = inbox[c, :lines, :]
-        block = jnp.concatenate([both[:, i * latent : (i + 1) * latent] for i in range(pack)], axis=0)
-        rows_out[c * row_count : (c + 1) * row_count, :] = block
-        project(block, 1, keys_out, c * row_count, 1.0)
-        meta = inbox[c, lines:, :].astype(F32)
-        labels.append(meta[2:3, :])
-        spots.append(jnp.where(meta[0:1, :] == ctx.astype(F32), meta[1:2, :] + (c * capacity), -1.0))
+    groups = [range(c, min(c + 3, shards)) for c in range(0, shards, 3)]
+    for group in groups:
+        blocks = []
+        for c in group:
+            arrival(c).wait_recv()
+            both = inbox[c, :lines, :]
+            blocks += [both[:, i * latent : (i + 1) * latent] for i in range(pack)]
+            meta = inbox[c, lines:, :].astype(F32)
+            labels.append(meta[2:3, :])
+            spots.append(jnp.where(meta[0:1, :] == ctx.astype(F32), meta[1:2, :] + (c * capacity), -1.0))
+        block = jnp.concatenate(blocks, axis=0)
+        start = group[0] * row_count
+        rows_out[start : start + block.shape[0], :] = block
+        project(block, 1, keys_out, start, 1.0)
     label = jnp.concatenate(labels, axis=1)
     spot = jnp.concatenate(spots, axis=1).astype(jnp.int32)
     taken = spot == iota((slots, spot.shape[1]), 0)

time: 13.8 us -> 13.8 us (level)
  no operation moved by 1% of the time
where the time goes in v6:
time: 13.8 us; the launch traced here: 13.7 us
  Pallas kernels  13.6 us (99%)
    pallas_call x1, Pallas kernels, on_device(): pl.pallas_call(functools.partial(encode_kernel, shards, frame_count, piec...  11 us
    pallas_call x1, Pallas kernels, on_device(): pl.pallas_call(attend_kernel, out_shape=jax.ShapeDtypeStruct((slots, colu...  2.64 us

profile of v6, /device:TPU:1, one launch (start us, length us, event | category | flops | bytes accessed | tf_op | source)
XLA Modules:
  0.0 13.7 jit_solution(10723370100323595827)
XLA Ops:
  0.0 11.0 %shard_map.82 = (bf16[2,3,64,512]{3,2,1,0:T(8,128)(2,1)S(1)}, bf16[512,64]{1,0:T(8,128)(2,1)S(1)}, bf16[192,1024]{1,0:T(8,128)(2,1)S(1)}, bf16[512,1024]{1,0:T(8,128)(2,1)S(1)}, f32[192,512]{1,0:T(8,128)S(1)}) custom-call(bf16[512,512]{1,0:T(8,128)(2,1)} %bitcast.7, bf16[3,512,512]{2,1,0:T(8,128)(2,1)} %conv_hbm.1, bf16[16,512]{1,0:T(8,128)(2,1)} %bitcast.9, ...), custom_call_target="tpu_custom_call" | custom-call | tf_op jit(solution)/shard_map/pallas_call | solution.py:302
  11.0 2.6 %shard_map.83 = bf16[192,1024]{1,0:T(8,128)(2,1)} custom-call(bf16[2,3,64,512]{3,2,1,0:T(8,128)(2,1)S(1)} %get-tuple-element.10.weff_ref, bf16[512,64]{1,0:T(8,128)(2,1)S(1)} %get-tuple-element.11.rows_ref, bf16[192,1024]{1,0:T(8,128)(2,1)S(1)} %get-tuple-element.12.queries_ref, bf16[512,1024]{1,0:T(8,128)(2,1)S(1)} %get-tuple-element.13.keys_ref, ...), custom_call_target="tpu_custom_call" | custom-call | tf_op jit(solution)/shard_map/pallas_call | solution.py:347
